TPU v7x, 32 devices: a whole 2x2x4 slice. The times are simulated.
32 devices in a mesh: win: 2 (over x), row: 16 (over z, y, core).
Axes of the slice: x: 2, y: 2, z: 4, core: 2. Of those that a mesh axis runs over, the one named last changes fastest.
Arguments:
- mask_field: float32 [2, 4096, 128], P(None, ('win', 'row')), parts along dimension 1, may hold values from -6 to 6
- target: int32 [4096, 128], P(('win', 'row')), parts along dimension 0, may hold values 0 or 1
- kernel_taps: float32 [24, 2, 128, 128], replicated, may hold values from -0.046875 to 0.046875
- kernel_radii: int32 [24], replicated, may hold values from 16 to 64, as said below
- kernel_group: int32 [24], replicated, may hold values from 0 to 2, as said below
- kernel_weight: float32 [24], replicated, may hold values from 0.1 to 1
Outputs:
- resist: float32 [3, 4096, 128], P(None, ('win', 'row')), parts along dimension 1
- gradient: float32 [2, 4096, 128], P(None, ('win', 'row')), parts along dimension 1
There are 2 independent parts, one for each index of `win`. A program takes and returns all parts, laid end to end along the dimension named above; an argument that names none is the same for every part. Nothing has to cross between parts.
Inputs may be any that keep to these rules, and one draw needn't show every extreme that they name: `kernel_radii`: every radius lies in 16 to 64; some kernel has radius exactly 64 and some exactly 16. `kernel_group`: every one of the 3 process conditions holds at least one kernel.
All inputs are finite; a program needn't handle non-finite values. No bound on the sum of `target` on one device may be relied on, other than what follows from the above.
Results may differ from a plain program's by a relative error of at most 0.0003.
Values sent between devices are 32-bit elements; how exact they have to be, the bound alone decides.
A program may use at most 128 MiB of HBM per device.

v0:
```python
import numpy as np

import jax
import jax.numpy as jnp
from jax import lax
from jax.experimental import pallas as pl
from jax.experimental.pallas import tpu as pltpu
from jax.sharding import PartitionSpec as P

RMAX = 64
GROUPS = 3
STEEPNESS = 1.0
THRESHOLD = 2.0
UNROLL = (4, 6, 6)
MESH = pl.DeviceIdType.MESH


def split_np(table):
    high = table.astype(jnp.bfloat16)
    low = (table - high.astype(np.float64)).astype(jnp.bfloat16)
    return high, low


def angles(points, grid):
    freqs = np.arange(grid // 2, dtype=np.int64)
    turns = (points.astype(np.int64)[:, None] * (2 * freqs[None, :] + 1)) % (2 * grid)
    return turns.astype(np.float64) * (np.pi / grid)


def tap_like(count):
    return np.arange(count) - RMAX


def tables(rows, cols):
    taps = 2 * RMAX
    grid_rows, grid_cols = rows + taps, cols + taps
    tap = np.arange(taps) - RMAX
    own, ext, col = tap_like(rows), np.arange(grid_rows) - 2 * RMAX, tap_like(cols)

    def right(points, grid):
        ang = angles(points, grid)
        high, low = split_np(np.concatenate([np.cos(ang), np.sin(ang)], 1))
        return np.stack([np.concatenate([high, high], 0), np.concatenate([low, low], 0)])

    def left(points, grid, deep):
        ang = angles(points, grid).T
        high, low = split_np(np.concatenate([np.cos(ang), np.sin(ang)], 0))
        if deep:
            high, low = np.concatenate([high, high], 1), np.concatenate([low, low], 1)
        return np.concatenate([high, low], 0)

    def back_left(points, grid):
        ang = angles(points, grid)
        high, low = split_np(np.concatenate([np.cos(ang), np.sin(ang)], 1) / grid)
        return np.concatenate([high, low], 0)

    def back_right(points, grid):
        ang = angles(points, grid).T
        high, low = split_np(np.concatenate([np.cos(ang), np.sin(ang)], 0) / grid)
        return np.concatenate([high, low], 1)

    return (
        right(tap, grid_cols),
        right(col, grid_cols),
        left(tap, grid_rows, True),
        left(own, grid_rows, True),
        left(ext, grid_rows, False),
        back_left(own, grid_rows),
        back_left(ext, grid_rows),
        back_right(col, grid_cols),
    )


def resist_of(intensity):
    return jax.nn.sigmoid(STEEPNESS * (intensity - THRESHOLD))


def dot(a, b):
    return lax.dot_general(a, b, (((1,), (0,)), ((), ())), preferred_element_type=jnp.float32)


def split(value):
    high = value.astype(jnp.bfloat16)
    low = (value - high.astype(jnp.float32)).astype(jnp.bfloat16)
    return high, low


def col_transform(pair, table):
    high, low = split(pair)
    data = jnp.concatenate([high, low], axis=1)
    return dot(data, table[0]) + dot(data, table[1])


def fold(value):
    half = value.shape[0] // 2
    return value[:half] + value[half:]


def row_transform(value, table):
    high, low = split(value)
    return fold(dot(table, jnp.concatenate([high, low], axis=0)))


def row_transform_wide(value, table):
    high, low = split(value)
    return fold(dot(table, high)) + dot(table[: table.shape[0] // 2], low)


def quadrants(real, imag):
    g, f = real.shape[0] // 2, real.shape[1] // 2

    def parts(v):
        cp, cq, sp, sq = v[:g, :f], v[:g, f:], v[g:, :f], v[g:, f:]
        return cp - sq, sp + cq, cp + sq, sp - cq

    e1r, e2r, e3r, e4r = parts(real)
    e1i, e2i, e3i, e4i = parts(imag)
    return (
        (e1r + e2i, e1i - e2r),
        (e1r - e2i, e1i + e2r),
        (e3r + e4i, e3i - e4r),
        (e3r - e4i, e3i + e4r),
    )


def inverse(quads, row_table, col_table):
    (pr, pi), (mr, mi), (qr, qi), (nr, ni) = quads
    sr, dr, tr, er = pr + mr, pr - mr, qr + nr, qr - nr
    si, di, ti, ei = pi + mi, pi - mi, qi + ni, qi - ni

    def stack(a, b, c, d):
        return jnp.concatenate(
            [jnp.concatenate([a, b], axis=1), jnp.concatenate([c, d], axis=1)], axis=0
        )

    real = stack(sr + tr, ei - di, -di - ei, tr - sr)
    imag = stack(si + ti, dr - er, dr + er, ti - si)
    half = jnp.concatenate(
        [row_transform_wide(real, row_table), row_transform_wide(imag, row_table)], axis=0
    )
    high, low = split(half)
    both = fold(dot(jnp.concatenate([high, low], axis=0), col_table))
    width = both.shape[1] // 2
    return both[:, :width] + both[:, width:]


def body(
    radii_ref,
    group_ref,
    weight_ref,
    taps_hbm,
    mask_hbm,
    target_hbm,
    *refs,
):
    table_hbm, refs = refs[:8], refs[8:]
    power_ref, own_ref, rim_ref = refs[:3]
    spec, fields, acc, slopes, taps_ref, ext_ref, target_ref, adj, rims = refs[3:12]
    table_ref, refs = refs[12:20], refs[20:]
    tap_sem, load_sem, send_sem, recv_sem = refs
    tap_col, own_col, tap_row, own_row, ext_row, back_own, back_ext, back_col = table_ref
    kernels, _, taps, _ = taps_hbm.shape
    rows, cols = target_hbm.shape
    me, count = lax.axis_index("row"), lax.axis_size("row")
    has_prev, has_next = me > 0, me < count - 1
    prev_id = {"row": lax.rem(me + count - 1, count)}
    next_id = {"row": lax.rem(me + 1, count)}

    def load(src, dst, slot):
        return pltpu.make_async_copy(src, dst, load_sem.at[slot])

    def tap_load(k):
        return pltpu.make_async_copy(taps_hbm.at[k], taps_ref.at[k], tap_sem.at[k])

    loads = [load(src, dst, i) for i, (src, dst) in enumerate(zip(table_hbm, table_ref))]
    load_mask = load(mask_hbm, ext_ref.at[:, pl.ds(RMAX, rows)], 8)
    load_target = load(target_hbm, target_ref, 9)
    loads[0].start()
    loads[2].start()

    def start_tap(k, carry):
        tap_load(k).start()
        return carry

    lax.fori_loop(0, kernels, start_tap, 0)
    load_mask.start()
    load_target.start()
    for i in (1, 3, 4, 5, 6, 7):
        loads[i].start()

    barrier = pltpu.get_barrier_semaphore()

    @pl.when(has_prev)
    def _():
        pl.semaphore_signal(barrier, inc=1, device_id=prev_id, device_id_type=MESH)

    @pl.when(has_next)
    def _():
        pl.semaphore_signal(barrier, inc=1, device_id=next_id, device_id_type=MESH)

    pl.semaphore_wait(barrier, has_prev.astype(jnp.int32) + has_next.astype(jnp.int32))

    def exchange(first, src_up, dst_up, src_down, dst_down):
        down = pltpu.make_async_remote_copy(
            src_ref=src_down,
            dst_ref=dst_down,
            send_sem=send_sem.at[first],
            recv_sem=recv_sem.at[first],
            device_id=next_id,
            device_id_type=MESH,
        )
        up = pltpu.make_async_remote_copy(
            src_ref=src_up,
            dst_ref=dst_up,
            send_sem=send_sem.at[first + 1],
            recv_sem=recv_sem.at[first + 1],
            device_id=prev_id,
            device_id_type=MESH,
        )
        return up, down

    def start_both(pair):
        up, down = pair

        @pl.when(has_next)
        def _():
            down.start()

        @pl.when(has_prev)
        def _():
            up.start()

    def wait_both(pair):
        up, down = pair

        @pl.when(has_prev)
        def _():
            up.wait_send()
            down.wait_recv()

        @pl.when(has_next)
        def _():
            down.wait_send()
            up.wait_recv()

    halo = exchange(
        0,
        mask_hbm.at[:, pl.ds(0, RMAX)],
        ext_ref.at[:, pl.ds(RMAX + rows, RMAX)],
        mask_hbm.at[:, pl.ds(rows - RMAX, RMAX)],
        ext_ref.at[:, pl.ds(0, RMAX)],
    )
    start_both(halo)

    @pl.when(jnp.logical_not(has_prev))
    def _():
        ext_ref[:, :RMAX] = jnp.zeros_like(ext_ref[:, :RMAX])
        rims[0] = jnp.zeros_like(rims[0])

    @pl.when(jnp.logical_not(has_next))
    def _():
        ext_ref[:, RMAX + rows :] = jnp.zeros_like(ext_ref[:, RMAX + rows :])
        rims[1] = jnp.zeros_like(rims[1])

    loads[0].wait()
    loads[2].wait()

    def spectrum(k, carry):
        tap_load(k).wait()
        radius = radii_ref[k]
        a = lax.broadcasted_iota(jnp.int32, (taps, taps), 0) - RMAX
        b = lax.broadcasted_iota(jnp.int32, (taps, taps), 1) - RMAX
        inside = (a >= -radius) & (a < radius) & (b >= -radius) & (b < radius)
        pair = jnp.concatenate(
            [jnp.where(inside, taps_ref[k, 0], 0.0), jnp.where(inside, taps_ref[k, 1], 0.0)], axis=0
        )
        half = col_transform(pair, tap_col)
        real = row_transform(half[:taps], tap_row[...])
        imag = row_transform(half[taps:], tap_row[...])
        for q, (re, im) in enumerate(quadrants(real, imag)):
            spec[k, 2 * q] = re
            spec[k, 2 * q + 1] = im
        return carry

    lax.fori_loop(0, kernels, spectrum, 0, unroll=UNROLL[0])

    load_mask.wait()
    load_target.wait()
    for i in (1, 3, 4, 5, 6, 7):
        loads[i].wait()
    wait_both(halo)

    ext = ext_ref.shape[1]
    half = col_transform(jnp.concatenate([ext_ref[0], ext_ref[1]], axis=0), own_col)
    real = row_transform_wide(half[:ext], ext_row[...])
    imag = row_transform_wide(half[ext:], ext_row[...])
    for q, (re, im) in enumerate(quadrants(real, imag)):
        acc[2 * q] = re
        acc[2 * q + 1] = im

    power_ref[...] = jnp.zeros_like(power_ref)

    def mixed(k, g):
        return jnp.where(group_ref[k] == g, weight_ref[k], 0.0)

    def forward(k, carry):
        quads = []
        for q in range(4):
            xr, xi = spec[k, 2 * q], spec[k, 2 * q + 1]
            mr, mi = acc[2 * q], acc[2 * q + 1]
            quads.append((xr * mr - xi * mi, xr * mi + xi * mr))
        field = inverse(quads, back_own[...], back_col[...])
        fields[k] = field
        power = field[:rows] * field[:rows] + field[rows:] * field[rows:]
        for g in range(GROUPS):
            power_ref[g] += mixed(k, g) * power
        return carry

    lax.fori_loop(0, kernels, forward, 0, unroll=UNROLL[1])

    target = target_ref[...].astype(jnp.float32)
    for g in range(GROUPS):
        resist = resist_of(power_ref[g])
        slopes[g] = 2.0 * (resist - target) * resist * (1.0 - resist) * STEEPNESS
    acc[...] = jnp.zeros_like(acc)

    def backward(k, carry):
        factor = sum(2.0 * mixed(k, g) * slopes[g] for g in range(GROUPS))
        field = fields[k]
        cot = jnp.concatenate([factor * field[:rows], factor * field[rows:]], axis=0)
        half = col_transform(cot, own_col)
        real = row_transform(half[:rows], own_row[...])
        imag = row_transform(half[rows:], own_row[...])
        for q, (wr, wi) in enumerate(quadrants(real, imag)):
            xr, xi = spec[k, 2 * q], spec[k, 2 * q + 1]
            acc[2 * q] += xr * wr + xi * wi
            acc[2 * q + 1] += xr * wi - xi * wr
        return carry

    lax.fori_loop(0, kernels, backward, 0, unroll=UNROLL[2])
    quads = [(acc[2 * q], acc[2 * q + 1]) for q in range(4)]
    adjoint = inverse(quads, back_ext[...], back_col[...])
    adj[0] = adjoint[:ext]
    adj[1] = adjoint[ext:]
    back = exchange(
        2,
        adj.at[:, pl.ds(0, RMAX)],
        rims.at[1],
        adj.at[:, pl.ds(RMAX + rows, RMAX)],
        rims.at[0],
    )
    start_both(back)
    own_ref[...] = adj[:, RMAX : RMAX + rows]
    if rows > 2 * RMAX:
        rim_ref[...] = jnp.zeros_like(rim_ref)
    wait_both(back)
    rim_ref[:, :RMAX] = rims[0]
    rim_ref[:, rows - RMAX :] = rims[1]


def finish(power_ref, own_ref, rim_ref, resist_ref, grad_ref):
    resist_ref[...] = resist_of(power_ref[...])
    grad_ref[...] = own_ref[...] + rim_ref[...]


def on_device(mask_field, target, kernel_taps, kernel_radii, kernel_group, kernel_weight):
    rows, cols = target.shape
    kernels, _, taps, _ = kernel_taps.shape
    grid_rows, grid_cols = rows + taps, cols + taps
    consts = [jnp.asarray(t) for t in tables(rows, cols)]
    vmem = pl.BlockSpec(memory_space=pltpu.VMEM)
    smem = pl.BlockSpec(memory_space=pltpu.SMEM)
    hbm = pl.BlockSpec(memory_space=pltpu.HBM)
    plane = (grid_rows // 2, grid_cols // 2)
    intensity, own, rim = pl.pallas_call(
        body,
        out_shape=(
            jax.ShapeDtypeStruct((GROUPS, rows, cols), jnp.float32),
            jax.ShapeDtypeStruct((2, rows, cols), jnp.float32),
            jax.ShapeDtypeStruct((2, rows, cols), jnp.float32),
        ),
        in_specs=[smem] * 3 + [hbm] * (3 + len(consts)),
        out_specs=(vmem, vmem, vmem),
        scratch_shapes=[
            pltpu.VMEM((kernels, 8) + plane, jnp.float32),
            pltpu.VMEM((kernels, 2 * rows, cols), jnp.float32),
            pltpu.VMEM((8,) + plane, jnp.float32),
            pltpu.VMEM((GROUPS, rows, cols), jnp.float32),
            pltpu.VMEM(kernel_taps.shape, jnp.float32),
            pltpu.VMEM((2, grid_rows, cols), jnp.float32),
            pltpu.VMEM((rows, cols), jnp.int32),
            pltpu.VMEM((2, grid_rows, cols), jnp.float32),
            pltpu.VMEM((2, 2, RMAX, cols), jnp.float32),
        ]
        + [pltpu.VMEM(t.shape, t.dtype) for t in consts]
        + [
            pltpu.SemaphoreType.DMA((kernels,)),
            pltpu.SemaphoreType.DMA((10,)),
            pltpu.SemaphoreType.DMA((4,)),
            pltpu.SemaphoreType.DMA((4,)),
        ],
        compiler_params=pltpu.CompilerParams(
            vmem_limit_bytes=56 * 1024 * 1024, collective_id=0, has_side_effects=True
        ),
        name="litho",
    )(kernel_radii, kernel_group, kernel_weight, kernel_taps, mask_field, target, *consts)
    return pl.pallas_call(
        finish,
        out_shape=(
            jax.ShapeDtypeStruct((GROUPS, rows, cols), jnp.float32),
            jax.ShapeDtypeStruct((2, rows, cols), jnp.float32),
        ),
        in_specs=[vmem] * 3,
        out_specs=(vmem, vmem),
        name="finish",
    )(intensity, own, rim)


def solution(mesh):
    in_specs = (P(None, ("win", "row"), None), P(("win", "row"), None), P(), P(), P(), P())
    out_specs = (P(None, ("win", "row"), None), P(None, ("win", "row"), None))
    return jax.shard_map(
        on_device, mesh=mesh, in_specs=in_specs, out_specs=out_specs, check_vma=False
    )
```

profile of v0, /device:TPU:1, one launch (start us, length us, event | category | flops | bytes accessed | tf_op | source)
XLA Modules:
  0.0 44.3 jit_solution(4553975480527772993)
XLA Ops:
  0.6 41.8 %litho.1 = (f32[3,128,128]{2,1,0:T(8,128)}, f32[2,128,128]{2,1,0:T(8,128)}, f32[2,128,128]{2,1,0:T(8,128)}) custom-call(s32[24]{0:T(128)} %radii_ref.1, s32[24]{0:T(128)} %group_ref.1, f32[24]{0:T(128)} %weight_ref.1, f32[24,2,128,128]{3,2,1,0:T(8,128)} %taps_hbm.1, f32[2,128,128]{2,1,0:T(8,128)} %mask_hbm.1, s32[128,128]{1,0:T(8,128)} %target_hbm.1, ...), custom_call_target="tpu_custom_call" | custom-call | tf_op jit(solution)/shard_map/litho/pallas_call | solution.py:375
  42.4 1.8 %finish.1 = (f32[3,128,128]{2,1,0:T(8,128)}, f32[2,128,128]{2,1,0:T(8,128)}) custom-call(f32[3,128,128]{2,1,0:T(8,128)} %get-tuple-element.5.power_ref, f32[2,128,128]{2,1,0:T(8,128)} %get-tuple-element.6.own_ref, f32[2,128,128]{2,1,0:T(8,128)} %get-tuple-element.7.rim_ref), custom_call_target="tpu_custom_call" | custom-call | tf_op jit(solution)/shard_map/finish/pallas_call | solution.py:407
where the time goes:
time: 44.4 us; the launch traced here: 44.3 us
  Pallas kernels  43.6 us (98%)
  between operations  0.64 us (1%)
    pallas_call x1, Pallas kernels, on_device(): pl.pallas_call(body, out_shape=(jax.ShapeDtypeStruct((GROUPS, rows, cols)...  41.8 us
    pallas_call x1, Pallas kernels, on_device(): pl.pallas_call(finish, out_shape=(jax.ShapeDtypeStruct((GROUPS, rows, col...  1.81 us

commit v1 on v0

--- a/solution.py
+++ b/solution.py
@@ -12,6 +12,7 @@
 STEEPNESS = 1.0
 THRESHOLD = 2.0
 UNROLL = (4, 6, 6)
+TABLES = 11
 MESH = pl.DeviceIdType.MESH
 
 
@@ -21,53 +22,65 @@
     return high, low
 
 
-def angles(points, grid):
+def angles(twice, grid):
     freqs = np.arange(grid // 2, dtype=np.int64)
-    turns = (points.astype(np.int64)[:, None] * (2 * freqs[None, :] + 1)) % (2 * grid)
-    return turns.astype(np.float64) * (np.pi / grid)
-
-
-def tap_like(count):
-    return np.arange(count) - RMAX
+    turns = (twice.astype(np.int64)[:, None] * (2 * freqs[None, :] + 1)) % (4 * grid)
+    return turns.astype(np.float64) * (np.pi / (2 * grid))
+
+
+def halves(count):
+    return 2 * np.arange(count // 2) + 1
 
 
 def tables(rows, cols):
     taps = 2 * RMAX
     grid_rows, grid_cols = rows + taps, cols + taps
-    tap = np.arange(taps) - RMAX
-    own, ext, col = tap_like(rows), np.arange(grid_rows) - 2 * RMAX, tap_like(cols)
+    tap, col = 2 * (np.arange(taps) - RMAX), 2 * (np.arange(cols) - RMAX)
+    ext = 2 * (np.arange(grid_rows) - RMAX - rows // 2)
 
     def right(points, grid):
         ang = angles(points, grid)
         high, low = split_np(np.concatenate([np.cos(ang), np.sin(ang)], 1))
-        return np.stack([np.concatenate([high, high], 0), np.concatenate([low, low], 0)])
-
-    def left(points, grid, deep):
+        return np.concatenate([high, high, low, low], 0)
+
+    def folded(points, grid, wave):
+        high, low = split_np(wave(angles(points, grid).T))
+        return np.concatenate([high, high, low, low], 1)
+
+    def left(points, grid):
         ang = angles(points, grid).T
-        high, low = split_np(np.concatenate([np.cos(ang), np.sin(ang)], 0))
-        if deep:
-            high, low = np.concatenate([high, high], 1), np.concatenate([low, low], 1)
-        return np.concatenate([high, low], 0)
+        return np.concatenate(split_np(np.concatenate([np.cos(ang), np.sin(ang)], 0)), 0)
+
+    def back_folded(points, grid, wave):
+        high, low = split_np(wave(angles(points, grid)) / grid)
+        return np.concatenate(
+            [np.concatenate([high, high], 1), np.concatenate([low, low], 1)], 0
+        )
 
     def back_left(points, grid):
         ang = angles(points, grid)
-        high, low = split_np(np.concatenate([np.cos(ang), np.sin(ang)], 1) / grid)
-        return np.concatenate([high, low], 0)
+        return np.concatenate(
+            split_np(np.concatenate([np.cos(ang), np.sin(ang)], 1) / grid), 0
+        )
 
     def back_right(points, grid):
         ang = angles(points, grid).T
         high, low = split_np(np.concatenate([np.cos(ang), np.sin(ang)], 0) / grid)
-        return np.concatenate([high, low], 1)
+        both = np.concatenate([high, low], 1)
+        return np.concatenate([both, both], 0)
 
     return (
         right(tap, grid_cols),
+        folded(halves(taps), grid_rows, np.cos),
+        folded(halves(taps), grid_rows, np.sin),
         right(col, grid_cols),
-        left(tap, grid_rows, True),
-        left(own, grid_rows, True),
-        left(ext, grid_rows, False),
-        back_left(own, grid_rows),
+        left(ext, grid_rows),
+        back_folded(halves(rows), grid_rows, np.cos),
+        back_folded(halves(rows), grid_rows, np.sin),
+        back_right(col, grid_cols),
+        folded(halves(rows), grid_rows, np.cos),
+        folded(halves(rows), grid_rows, np.sin),
         back_left(ext, grid_rows),
-        back_right(col, grid_cols),
     )
 
 
@@ -85,20 +98,90 @@
     return high, low
 
 
-def col_transform(pair, table):
-    high, low = split(pair)
-    data = jnp.concatenate([high, low], axis=1)
-    return dot(data, table[0]) + dot(data, table[1])
-
-
 def fold(value):
     half = value.shape[0] // 2
     return value[:half] + value[half:]
 
 
-def row_transform(value, table):
-    high, low = split(value)
-    return fold(dot(table, jnp.concatenate([high, low], axis=0)))
+def flip(value):
+    tiles = value.reshape(value.shape[0] // 8, 8, value.shape[1])
+    spot = lax.broadcasted_iota(jnp.int32, tiles.shape, 1)
+    for step in (4, 2, 1):
+        down = pltpu.roll(tiles, step, 1)
+        up = down if step == 4 else pltpu.roll(tiles, 8 - step, 1)
+        tiles = down if step == 4 else jnp.where((spot & step) == 0, up, down)
+    return jnp.concatenate([tiles[i] for i in range(tiles.shape[0] - 1, -1, -1)], axis=0)
+
+
+def fold_rows(plus_real, minus_real, plus_imag, minus_imag):
+    return jnp.concatenate(
+        [
+            plus_real + minus_real,
+            plus_real - minus_real,
+            plus_imag + minus_imag,
+            plus_imag - minus_imag,
+        ],
+        axis=0,
+    )
+
+
+def col_transform(rows, table):
+    high, low = split(rows)
+    return dot(jnp.concatenate([high, low, high, low], axis=1), table)
+
+
+def signed(real, imag):
+    width = real.shape[1] // 2
+    rc, rs, ic, js = real[:, :width], real[:, width:], imag[:, :width], imag[:, width:]
+    return jnp.concatenate([rc + js, ic - rs, rc - js, ic + rs], axis=1)
+
+
+def unsigned(value):
+    width = value.shape[1] // 4
+    pr, pi, mr, mi = (value[:, i * width : (i + 1) * width] for i in range(4))
+    return (
+        jnp.concatenate([pr + mr, mi - pi], axis=1),
+        jnp.concatenate([pi + mi, pr - mr], axis=1),
+    )
+
+
+def quadrants(cos_part, sin_part):
+    width = cos_part.shape[1] // 4
+    quads = []
+    for s in range(2):
+        real, imag = slice(2 * s * width, (2 * s + 1) * width), slice((2 * s + 1) * width, (2 * s + 2) * width)
+        cr, ci, sr, si = cos_part[:, real], cos_part[:, imag], sin_part[:, real], sin_part[:, imag]
+        quads.append((cr + si, ci - sr))
+        quads.append((cr - si, ci + sr))
+    return quads
+
+
+def waves(quads):
+    (ar, ai), (br, bi), (cr, ci), (dr, di) = quads
+    cos_part = jnp.concatenate([ar + br, ai + bi, cr + dr, ci + di], axis=1)
+    sin_part = jnp.concatenate([bi - ai, ar - br, di - ci, cr - dr], axis=1)
+    return cos_part, sin_part
+
+
+def transform(rows, col_table, cos_table, sin_table):
+    half = col_transform(rows, col_table)
+    quarter = half.shape[0] // 4
+    er, orr, ei, oi = (half[i * quarter : (i + 1) * quarter] for i in range(4))
+
+    def along_rows(table, value):
+        high, low = split(value)
+        return dot(table, jnp.concatenate([high, low, high, low], axis=0))
+
+    return quadrants(
+        along_rows(cos_table, signed(er, ei)), along_rows(sin_table, signed(orr, oi))
+    )
+
+
+def col_inverse(rows, table):
+    high, low = split(rows)
+    both = dot(jnp.concatenate([high, low], axis=1), table)
+    width = both.shape[1] // 2
+    return both[:, :width] + both[:, width:]
 
 
 def row_transform_wide(value, table):
@@ -106,42 +189,25 @@
     return fold(dot(table, high)) + dot(table[: table.shape[0] // 2], low)
 
 
-def quadrants(real, imag):
-    g, f = real.shape[0] // 2, real.shape[1] // 2
-
-    def parts(v):
-        cp, cq, sp, sq = v[:g, :f], v[:g, f:], v[g:, :f], v[g:, f:]
-        return cp - sq, sp + cq, cp + sq, sp - cq
-
-    e1r, e2r, e3r, e4r = parts(real)
-    e1i, e2i, e3i, e4i = parts(imag)
-    return (
-        (e1r + e2i, e1i - e2r),
-        (e1r - e2i, e1i + e2r),
-        (e3r + e4i, e3i - e4r),
-        (e3r - e4i, e3i + e4r),
-    )
-
-
-def inverse(quads, row_table, col_table):
-    (pr, pi), (mr, mi), (qr, qi), (nr, ni) = quads
-    sr, dr, tr, er = pr + mr, pr - mr, qr + nr, qr - nr
-    si, di, ti, ei = pi + mi, pi - mi, qi + ni, qi - ni
-
-    def stack(a, b, c, d):
-        return jnp.concatenate(
-            [jnp.concatenate([a, b], axis=1), jnp.concatenate([c, d], axis=1)], axis=0
-        )
-
-    real = stack(sr + tr, ei - di, -di - ei, tr - sr)
-    imag = stack(si + ti, dr - er, dr + er, ti - si)
-    half = jnp.concatenate(
-        [row_transform_wide(real, row_table), row_transform_wide(imag, row_table)], axis=0
-    )
-    high, low = split(half)
-    both = fold(dot(jnp.concatenate([high, low], axis=0), col_table))
-    width = both.shape[1] // 2
-    return both[:, :width] + both[:, width:]
+def inverse_folded(quads, cos_table, sin_table, col_table):
+    cos_part, sin_part = waves(quads)
+
+    def along_rows(table, value):
+        high, low = split(value)
+        return fold(dot(table, jnp.concatenate([high, low], axis=0)))
+
+    er, ei = unsigned(along_rows(cos_table, cos_part))
+    orr, oi = unsigned(along_rows(sin_table, sin_part))
+    out = col_inverse(jnp.concatenate([er, orr, ei, oi], axis=0), col_table)
+    quarter = out.shape[0] // 4
+    er, orr, ei, oi = (out[i * quarter : (i + 1) * quarter] for i in range(4))
+    return jnp.concatenate([er + orr, er - orr, ei + oi, ei - oi], axis=0)
+
+
+def inverse_wide(quads, row_table, col_table):
+    cos_part, sin_part = waves(quads)
+    half = row_transform_wide(jnp.concatenate([cos_part, sin_part], axis=0), row_table)
+    return col_inverse(jnp.concatenate(unsigned(half), axis=0), col_table)
 
 
 def body(
@@ -153,12 +219,13 @@
     target_hbm,
     *refs,
 ):
-    table_hbm, refs = refs[:8], refs[8:]
-    power_ref, own_ref, rim_ref = refs[:3]
-    spec, fields, acc, slopes, taps_ref, ext_ref, target_ref, adj, rims = refs[3:12]
-    table_ref, refs = refs[12:20], refs[20:]
+    table_hbm, refs = refs[:TABLES], refs[TABLES:]
+    out_ref, own_ref, rim_ref = refs[:3]
+    spec, fields, acc, power_ref, slopes, taps_ref, ext_ref, target_ref, adj, rims = refs[3:13]
+    table_ref, refs = refs[13 : 13 + TABLES], refs[13 + TABLES :]
     tap_sem, load_sem, send_sem, recv_sem = refs
-    tap_col, own_col, tap_row, own_row, ext_row, back_own, back_ext, back_col = table_ref
+    tap_col, tap_cos, tap_sin, own_col, ext_row = table_ref[:5]
+    back_cos, back_sin, back_col, own_cos, own_sin, back_ext = table_ref[5:]
     kernels, _, taps, _ = taps_hbm.shape
     rows, cols = target_hbm.shape
     me, count = lax.axis_index("row"), lax.axis_size("row")
@@ -173,10 +240,10 @@
         return pltpu.make_async_copy(taps_hbm.at[k], taps_ref.at[k], tap_sem.at[k])
 
     loads = [load(src, dst, i) for i, (src, dst) in enumerate(zip(table_hbm, table_ref))]
-    load_mask = load(mask_hbm, ext_ref.at[:, pl.ds(RMAX, rows)], 8)
-    load_target = load(target_hbm, target_ref, 9)
-    loads[0].start()
-    loads[2].start()
+    load_mask = load(mask_hbm, ext_ref.at[:, pl.ds(RMAX, rows)], TABLES)
+    load_target = load(target_hbm, target_ref, TABLES + 1)
+    for i in range(3):
+        loads[i].start()
 
     def start_tap(k, carry):
         tap_load(k).start()
@@ -185,7 +252,7 @@
     lax.fori_loop(0, kernels, start_tap, 0)
     load_mask.start()
     load_target.start()
-    for i in (1, 3, 4, 5, 6, 7):
+    for i in range(3, TABLES):
         loads[i].start()
 
     barrier = pltpu.get_barrier_semaphore()
@@ -262,22 +329,21 @@
         ext_ref[:, RMAX + rows :] = jnp.zeros_like(ext_ref[:, RMAX + rows :])
         rims[1] = jnp.zeros_like(rims[1])
 
-    loads[0].wait()
-    loads[2].wait()
+    for i in range(3):
+        loads[i].wait()
 
     def spectrum(k, carry):
         tap_load(k).wait()
         radius = radii_ref[k]
-        a = lax.broadcasted_iota(jnp.int32, (taps, taps), 0) - RMAX
-        b = lax.broadcasted_iota(jnp.int32, (taps, taps), 1) - RMAX
-        inside = (a >= -radius) & (a < radius) & (b >= -radius) & (b < radius)
-        pair = jnp.concatenate(
-            [jnp.where(inside, taps_ref[k, 0], 0.0), jnp.where(inside, taps_ref[k, 1], 0.0)], axis=0
-        )
-        half = col_transform(pair, tap_col)
-        real = row_transform(half[:taps], tap_row[...])
-        imag = row_transform(half[taps:], tap_row[...])
-        for q, (re, im) in enumerate(quadrants(real, imag)):
+        a = lax.broadcasted_iota(jnp.int32, (RMAX, taps), 0)
+        b = lax.broadcasted_iota(jnp.int32, (RMAX, taps), 1) - RMAX
+        inside = (a < radius) & (b >= -radius) & (b < radius)
+        parts = []
+        for part in range(2):
+            parts.append(jnp.where(inside, taps_ref[k, part, RMAX:], 0.0))
+            parts.append(jnp.where(inside, flip(taps_ref[k, part, :RMAX]), 0.0))
+        quads = transform(fold_rows(*parts), tap_col[...], tap_cos[...], tap_sin[...])
+        for q, (re, im) in enumerate(quads):
             spec[k, 2 * q] = re
             spec[k, 2 * q + 1] = im
         return carry
@@ -286,15 +352,15 @@
 
     load_mask.wait()
     load_target.wait()
-    for i in (1, 3, 4, 5, 6, 7):
+    for i in range(3, TABLES):
         loads[i].wait()
     wait_both(halo)
 
     ext = ext_ref.shape[1]
-    half = col_transform(jnp.concatenate([ext_ref[0], ext_ref[1]], axis=0), own_col)
-    real = row_transform_wide(half[:ext], ext_row[...])
-    imag = row_transform_wide(half[ext:], ext_row[...])
-    for q, (re, im) in enumerate(quadrants(real, imag)):
+    half = col_transform(jnp.concatenate([ext_ref[0], ext_ref[1]], axis=0), own_col[...])
+    both = row_transform_wide(signed(half[:ext], half[ext:]), ext_row[...])
+    middle = both.shape[0] // 2
+    for q, (re, im) in enumerate(quadrants(both[:middle], both[middle:])):
         acc[2 * q] = re
         acc[2 * q + 1] = im
 
@@ -309,7 +375,7 @@
             xr, xi = spec[k, 2 * q], spec[k, 2 * q + 1]
             mr, mi = acc[2 * q], acc[2 * q + 1]
             quads.append((xr * mr - xi * mi, xr * mi + xi * mr))
-        field = inverse(quads, back_own[...], back_col[...])
+        field = inverse_folded(quads, back_cos[...], back_sin[...], back_col[...])
         fields[k] = field
         power = field[:rows] * field[:rows] + field[rows:] * field[rows:]
         for g in range(GROUPS):
@@ -318,20 +384,25 @@
 
     lax.fori_loop(0, kernels, forward, 0, unroll=UNROLL[1])
 
+    half_rows = rows // 2
     target = target_ref[...].astype(jnp.float32)
+    target = jnp.concatenate([target[half_rows:], flip(target[:half_rows])], axis=0)
     for g in range(GROUPS):
-        resist = resist_of(power_ref[g])
+        power = power_ref[g]
+        out_ref[g] = jnp.concatenate([flip(power[half_rows:]), power[:half_rows]], axis=0)
+        resist = resist_of(power)
         slopes[g] = 2.0 * (resist - target) * resist * (1.0 - resist) * STEEPNESS
     acc[...] = jnp.zeros_like(acc)
 
     def backward(k, carry):
-        factor = sum(2.0 * mixed(k, g) * slopes[g] for g in range(GROUPS))
-        field = fields[k]
-        cot = jnp.concatenate([factor * field[:rows], factor * field[rows:]], axis=0)
-        half = col_transform(cot, own_col)
-        real = row_transform(half[:rows], own_row[...])
-        imag = row_transform(half[rows:], own_row[...])
-        for q, (wr, wi) in enumerate(quadrants(real, imag)):
+        factor = (2.0 * weight_ref[k]) * slopes[group_ref[k]]
+        plus, minus = factor[:half_rows], factor[half_rows:]
+        parts = []
+        for part in range(2):
+            parts.append(plus * fields[k, part * rows : part * rows + half_rows])
+            parts.append(minus * fields[k, part * rows + half_rows : (part + 1) * rows])
+        quads = transform(fold_rows(*parts), own_col[...], own_cos[...], own_sin[...])
+        for q, (wr, wi) in enumerate(quads):
             xr, xi = spec[k, 2 * q], spec[k, 2 * q + 1]
             acc[2 * q] += xr * wr + xi * wi
             acc[2 * q + 1] += xr * wi - xi * wr
@@ -339,7 +410,7 @@
 
     lax.fori_loop(0, kernels, backward, 0, unroll=UNROLL[2])
     quads = [(acc[2 * q], acc[2 * q + 1]) for q in range(4)]
-    adjoint = inverse(quads, back_ext[...], back_col[...])
+    adjoint = inverse_wide(quads, back_ext[...], back_col[...])
     adj[0] = adjoint[:ext]
     adj[1] = adjoint[ext:]
     back = exchange(
@@ -386,6 +457,7 @@
             pltpu.VMEM((kernels, 2 * rows, cols), jnp.float32),
             pltpu.VMEM((8,) + plane, jnp.float32),
             pltpu.VMEM((GROUPS, rows, cols), jnp.float32),
+            pltpu.VMEM((GROUPS, rows, cols), jnp.float32),
             pltpu.VMEM(kernel_taps.shape, jnp.float32),
             pltpu.VMEM((2, grid_rows, cols), jnp.float32),
             pltpu.VMEM((rows, cols), jnp.int32),
@@ -395,7 +467,7 @@
         + [pltpu.VMEM(t.shape, t.dtype) for t in consts]
         + [
             pltpu.SemaphoreType.DMA((kernels,)),
-            pltpu.SemaphoreType.DMA((10,)),
+            pltpu.SemaphoreType.DMA((TABLES + 2,)),
             pltpu.SemaphoreType.DMA((4,)),
             pltpu.SemaphoreType.DMA((4,)),
         ],

time: 44.4 us -> 37.6 us (0.85)
  Pallas kernels: 43.6 us -> 36.8 us
    pallas_call x1, Pallas kernels: 41.8 us -> 35 us  [on_device(): pl.pallas_call(body, out_shape=(jax.ShapeDtypeStruct((GROUPS, rows, cols)...]
where the time goes in v1:
time: 37.6 us; the launch traced here: 37.5 us
  Pallas kernels  36.8 us (98%)
  between operations  0.64 us (2%)
    pallas_call x1, Pallas kernels, on_device(): pl.pallas_call(body, out_shape=(jax.ShapeDtypeStruct((GROUPS, rows, cols)...  35 us
    pallas_call x1, Pallas kernels, on_device(): pl.pallas_call(finish, out_shape=(jax.ShapeDtypeStruct((GROUPS, rows, col...  1.81 us

profile of v1, /device:TPU:1, one launch (start us, length us, event | category | flops | bytes accessed | tf_op | source)
XLA Modules:
  0.0 37.5 jit_solution(7371647649113643686)
XLA Ops:
  0.6 35.0 %litho.1 = (f32[3,128,128]{2,1,0:T(8,128)}, f32[2,128,128]{2,1,0:T(8,128)}, f32[2,128,128]{2,1,0:T(8,128)}) custom-call(s32[24]{0:T(128)} %radii_ref.1, s32[24]{0:T(128)} %group_ref.1, f32[24]{0:T(128)} %weight_ref.1, f32[24,2,128,128]{3,2,1,0:T(8,128)} %taps_hbm.1, f32[2,128,128]{2,1,0:T(8,128)} %mask_hbm.1, s32[128,128]{1,0:T(8,128)} %target_hbm.1, ...), custom_call_target="tpu_custom_call" | custom-call | tf_op jit(solution)/shard_map/litho/pallas_call | solution.py:446
  35.6 1.8 %finish.1 = (f32[3,128,128]{2,1,0:T(8,128)}, f32[2,128,128]{2,1,0:T(8,128)}) custom-call(f32[3,128,128]{2,1,0:T(8,128)} %get-tuple-element.5.power_ref, f32[2,128,128]{2,1,0:T(8,128)} %get-tuple-element.6.own_ref, f32[2,128,128]{2,1,0:T(8,128)} %get-tuple-element.7.rim_ref), custom_call_target="tpu_custom_call" | custom-call | tf_op jit(solution)/shard_map/finish/pallas_call | solution.py:479

commit v2 on v1

--- a/solution.py
+++ b/solution.py
@@ -12,7 +12,7 @@
 STEEPNESS = 1.0
 THRESHOLD = 2.0
 UNROLL = (4, 6, 6)
-TABLES = 11
+TABLES = 13
 MESH = pl.DeviceIdType.MESH
 
 
@@ -32,55 +32,62 @@
     return 2 * np.arange(count // 2) + 1
 
 
+def grids(rows, cols):
+    return rows + 2 * RMAX, cols + RMAX
+
+
 def tables(rows, cols):
     taps = 2 * RMAX
-    grid_rows, grid_cols = rows + taps, cols + taps
-    tap, col = 2 * (np.arange(taps) - RMAX), 2 * (np.arange(cols) - RMAX)
-    ext = 2 * (np.arange(grid_rows) - RMAX - rows // 2)
-
-    def right(points, grid):
-        ang = angles(points, grid)
+    grid_rows, grid_cols = grids(rows, cols)
+    tap, own = 2 * (np.arange(taps) - RMAX), 2 * (np.arange(rows) - rows // 2)
+    ext = 2 * (np.arange(rows + taps) - RMAX - rows // 2)
+    col = 2 * (np.arange(cols) - cols // 2)
+
+    def right(points):
+        ang = angles(points, grid_rows)
         high, low = split_np(np.concatenate([np.cos(ang), np.sin(ang)], 1))
         return np.concatenate([high, high, low, low], 0)
 
-    def folded(points, grid, wave):
-        high, low = split_np(wave(angles(points, grid).T))
+    def back_right(points):
+        ang = angles(points, grid_rows).T
+        high, low = split_np(np.concatenate([np.cos(ang), np.sin(ang)], 0) / grid_rows)
+        both = np.concatenate([high, low], 1)
+        return np.concatenate([both, both], 0)
+
+    def folded(points, wave):
+        high, low = split_np(wave(angles(points, grid_cols).T))
         return np.concatenate([high, high, low, low], 1)
 
-    def left(points, grid):
-        ang = angles(points, grid).T
-        return np.concatenate(split_np(np.concatenate([np.cos(ang), np.sin(ang)], 0)), 0)
-
-    def back_folded(points, grid, wave):
-        high, low = split_np(wave(angles(points, grid)) / grid)
+    def back_folded(points, wave):
+        high, low = split_np(wave(angles(points, grid_cols)) / grid_cols)
         return np.concatenate(
             [np.concatenate([high, high], 1), np.concatenate([low, low], 1)], 0
         )
 
-    def back_left(points, grid):
-        ang = angles(points, grid)
-        return np.concatenate(
-            split_np(np.concatenate([np.cos(ang), np.sin(ang)], 1) / grid), 0
-        )
-
-    def back_right(points, grid):
-        ang = angles(points, grid).T
-        high, low = split_np(np.concatenate([np.cos(ang), np.sin(ang)], 0) / grid)
-        both = np.concatenate([high, low], 1)
-        return np.concatenate([both, both], 0)
+    def left(points):
+        ang = angles(points, grid_cols).T
+        high, low = split_np(np.concatenate([np.cos(ang), np.sin(ang)], 0))
+        return np.concatenate([high, high, low, low], 1)
+
+    def back_left(points):
+        ang = angles(points, grid_cols)
+        high, low = split_np(np.concatenate([np.cos(ang), np.sin(ang)], 1) / grid_cols)
+        return np.concatenate([high, high, low, low], 1)
 
     return (
-        right(tap, grid_cols),
-        folded(halves(taps), grid_rows, np.cos),
-        folded(halves(taps), grid_rows, np.sin),
-        right(col, grid_cols),
-        left(ext, grid_rows),
-        back_folded(halves(rows), grid_rows, np.cos),
-        back_folded(halves(rows), grid_rows, np.sin),
-        back_right(col, grid_cols),
-        folded(halves(rows), grid_rows, np.cos),
-        folded(halves(rows), grid_rows, np.sin),
-        back_left(ext, grid_rows),
+        right(tap),
+        folded(halves(taps), np.cos),
+        folded(halves(taps), np.sin),
+        right(ext),
+        left(col),
+        back_folded(halves(cols), np.cos),
+        back_folded(halves(cols), np.sin),
+        back_right(own),
+        right(own),
+        folded(halves(cols), np.cos),
+        folded(halves(cols), np.sin),
+        back_left(col),
+        back_right(ext),
     )
 
 
@@ -125,7 +132,7 @@
     )
 
 
-def col_transform(rows, table):
+def lane_transform(rows, table):
     high, low = split(rows)
     return dot(jnp.concatenate([high, low, high, low], axis=1), table)
 
@@ -163,51 +170,54 @@
     return cos_part, sin_part
 
 
-def transform(rows, col_table, cos_table, sin_table):
-    half = col_transform(rows, col_table)
+def transform(rows, lane_table, cos_table, sin_table):
+    half = lane_transform(rows, lane_table)
     quarter = half.shape[0] // 4
     er, orr, ei, oi = (half[i * quarter : (i + 1) * quarter] for i in range(4))
 
-    def along_rows(table, value):
+    def along_columns(table, value):
         high, low = split(value)
         return dot(table, jnp.concatenate([high, low, high, low], axis=0))
 
     return quadrants(
-        along_rows(cos_table, signed(er, ei)), along_rows(sin_table, signed(orr, oi))
-    )
-
-
-def col_inverse(rows, table):
+        along_columns(cos_table, signed(er, ei)), along_columns(sin_table, signed(orr, oi))
+    )
+
+
+def lane_inverse(rows, table):
     high, low = split(rows)
     both = dot(jnp.concatenate([high, low], axis=1), table)
     width = both.shape[1] // 2
     return both[:, :width] + both[:, width:]
 
 
-def row_transform_wide(value, table):
+def wide(table, value):
     high, low = split(value)
-    return fold(dot(table, high)) + dot(table[: table.shape[0] // 2], low)
-
-
-def inverse_folded(quads, cos_table, sin_table, col_table):
+    return dot(table, jnp.concatenate([high, low, high, low], axis=0))
+
+
+def inverse_folded(quads, cos_table, sin_table, lane_table):
     cos_part, sin_part = waves(quads)
 
-    def along_rows(table, value):
+    def along_columns(table, value):
         high, low = split(value)
         return fold(dot(table, jnp.concatenate([high, low], axis=0)))
 
-    er, ei = unsigned(along_rows(cos_table, cos_part))
-    orr, oi = unsigned(along_rows(sin_table, sin_part))
-    out = col_inverse(jnp.concatenate([er, orr, ei, oi], axis=0), col_table)
+    er, ei = unsigned(along_columns(cos_table, cos_part))
+    orr, oi = unsigned(along_columns(sin_table, sin_part))
+    out = lane_inverse(jnp.concatenate([er, orr, ei, oi], axis=0), lane_table)
     quarter = out.shape[0] // 4
     er, orr, ei, oi = (out[i * quarter : (i + 1) * quarter] for i in range(4))
     return jnp.concatenate([er + orr, er - orr, ei + oi, ei - oi], axis=0)
 
 
-def inverse_wide(quads, row_table, col_table):
+def inverse_wide(quads, left_table, lane_table):
     cos_part, sin_part = waves(quads)
-    half = row_transform_wide(jnp.concatenate([cos_part, sin_part], axis=0), row_table)
-    return col_inverse(jnp.concatenate(unsigned(half), axis=0), col_table)
+    half = wide(left_table, jnp.concatenate([cos_part, sin_part], axis=0))
+    high, low = split(jnp.concatenate(unsigned(half), axis=0))
+    both = dot(jnp.concatenate([high, low], axis=1), lane_table)
+    width = both.shape[1] // 2
+    return both[:, :width] + both[:, width:]
 
 
 def body(
@@ -224,8 +234,9 @@
     spec, fields, acc, power_ref, slopes, taps_ref, ext_ref, target_ref, adj, rims = refs[3:13]
     table_ref, refs = refs[13 : 13 + TABLES], refs[13 + TABLES :]
     tap_sem, load_sem, send_sem, recv_sem = refs
-    tap_col, tap_cos, tap_sin, own_col, ext_row = table_ref[:5]
-    back_cos, back_sin, back_col, own_cos, own_sin, back_ext = table_ref[5:]
+    tap_lane, tap_cos, tap_sin, ext_lane, mask_left = table_ref[:5]
+    back_cos, back_sin, back_own, own_lane, own_cos, own_sin = table_ref[5:11]
+    back_left, back_ext = table_ref[11:]
     kernels, _, taps, _ = taps_hbm.shape
     rows, cols = target_hbm.shape
     me, count = lax.axis_index("row"), lax.axis_size("row")
@@ -332,23 +343,29 @@
     for i in range(3):
         loads[i].wait()
 
-    def spectrum(k, carry):
-        tap_load(k).wait()
+    def spectrum(k):
         radius = radii_ref[k]
-        a = lax.broadcasted_iota(jnp.int32, (RMAX, taps), 0)
-        b = lax.broadcasted_iota(jnp.int32, (RMAX, taps), 1) - RMAX
-        inside = (a < radius) & (b >= -radius) & (b < radius)
+        b = lax.broadcasted_iota(jnp.int32, (RMAX, taps), 0)
+        a = lax.broadcasted_iota(jnp.int32, (RMAX, taps), 1) - RMAX
+        inside = (b < radius) & (a >= -radius) & (a < radius)
         parts = []
         for part in range(2):
-            parts.append(jnp.where(inside, taps_ref[k, part, RMAX:], 0.0))
-            parts.append(jnp.where(inside, flip(taps_ref[k, part, :RMAX]), 0.0))
-        quads = transform(fold_rows(*parts), tap_col[...], tap_cos[...], tap_sin[...])
+            turned = taps_ref[k, part].T
+            parts.append(jnp.where(inside, turned[RMAX:], 0.0))
+            parts.append(jnp.where(inside, flip(turned[:RMAX]), 0.0))
+        quads = transform(fold_rows(*parts), tap_lane[...], tap_cos[...], tap_sin[...])
         for q, (re, im) in enumerate(quads):
             spec[k, 2 * q] = re
             spec[k, 2 * q + 1] = im
+
+    def batch(step, carry):
+        for i in range(UNROLL[0]):
+            tap_load(step * UNROLL[0] + i).wait()
+        for i in range(UNROLL[0]):
+            spectrum(step * UNROLL[0] + i)
         return carry
 
-    lax.fori_loop(0, kernels, spectrum, 0, unroll=UNROLL[0])
+    lax.fori_loop(0, kernels // UNROLL[0], batch, 0)
 
     load_mask.wait()
     load_target.wait()
@@ -356,9 +373,9 @@
         loads[i].wait()
     wait_both(halo)
 
-    ext = ext_ref.shape[1]
-    half = col_transform(jnp.concatenate([ext_ref[0], ext_ref[1]], axis=0), own_col[...])
-    both = row_transform_wide(signed(half[:ext], half[ext:]), ext_row[...])
+    mask = jnp.concatenate([ext_ref[0].T, ext_ref[1].T], axis=0)
+    half = lane_transform(mask, ext_lane[...])
+    both = wide(mask_left[...], signed(half[:cols], half[cols:]))
     middle = both.shape[0] // 2
     for q, (re, im) in enumerate(quadrants(both[:middle], both[middle:])):
         acc[2 * q] = re
@@ -375,33 +392,33 @@
             xr, xi = spec[k, 2 * q], spec[k, 2 * q + 1]
             mr, mi = acc[2 * q], acc[2 * q + 1]
             quads.append((xr * mr - xi * mi, xr * mi + xi * mr))
-        field = inverse_folded(quads, back_cos[...], back_sin[...], back_col[...])
+        field = inverse_folded(quads, back_cos[...], back_sin[...], back_own[...])
         fields[k] = field
-        power = field[:rows] * field[:rows] + field[rows:] * field[rows:]
+        power = field[:cols] * field[:cols] + field[cols:] * field[cols:]
         for g in range(GROUPS):
             power_ref[g] += mixed(k, g) * power
         return carry
 
     lax.fori_loop(0, kernels, forward, 0, unroll=UNROLL[1])
 
-    half_rows = rows // 2
-    target = target_ref[...].astype(jnp.float32)
-    target = jnp.concatenate([target[half_rows:], flip(target[:half_rows])], axis=0)
+    middle = cols // 2
+    target = target_ref[...].astype(jnp.float32).T
+    target = jnp.concatenate([target[middle:], flip(target[:middle])], axis=0)
     for g in range(GROUPS):
         power = power_ref[g]
-        out_ref[g] = jnp.concatenate([flip(power[half_rows:]), power[:half_rows]], axis=0)
+        out_ref[g] = jnp.concatenate([flip(power[middle:]), power[:middle]], axis=0).T
         resist = resist_of(power)
         slopes[g] = 2.0 * (resist - target) * resist * (1.0 - resist) * STEEPNESS
     acc[...] = jnp.zeros_like(acc)
 
     def backward(k, carry):
         factor = (2.0 * weight_ref[k]) * slopes[group_ref[k]]
-        plus, minus = factor[:half_rows], factor[half_rows:]
+        plus, minus = factor[:middle], factor[middle:]
         parts = []
         for part in range(2):
-            parts.append(plus * fields[k, part * rows : part * rows + half_rows])
-            parts.append(minus * fields[k, part * rows + half_rows : (part + 1) * rows])
-        quads = transform(fold_rows(*parts), own_col[...], own_cos[...], own_sin[...])
+            parts.append(plus * fields[k, part * cols : part * cols + middle])
+            parts.append(minus * fields[k, part * cols + middle : (part + 1) * cols])
+        quads = transform(fold_rows(*parts), own_lane[...], own_cos[...], own_sin[...])
         for q, (wr, wi) in enumerate(quads):
             xr, xi = spec[k, 2 * q], spec[k, 2 * q + 1]
             acc[2 * q] += xr * wr + xi * wi
@@ -410,9 +427,9 @@
 
     lax.fori_loop(0, kernels, backward, 0, unroll=UNROLL[2])
     quads = [(acc[2 * q], acc[2 * q + 1]) for q in range(4)]
-    adjoint = inverse_wide(quads, back_ext[...], back_col[...])
-    adj[0] = adjoint[:ext]
-    adj[1] = adjoint[ext:]
+    adjoint = inverse_wide(quads, back_left[...], back_ext[...])
+    adj[0] = adjoint[:cols].T
+    adj[1] = adjoint[cols:].T
     back = exchange(
         2,
         adj.at[:, pl.ds(0, RMAX)],
@@ -437,12 +454,12 @@
 def on_device(mask_field, target, kernel_taps, kernel_radii, kernel_group, kernel_weight):
     rows, cols = target.shape
     kernels, _, taps, _ = kernel_taps.shape
-    grid_rows, grid_cols = rows + taps, cols + taps
+    grid_rows, grid_cols = grids(rows, cols)
     consts = [jnp.asarray(t) for t in tables(rows, cols)]
     vmem = pl.BlockSpec(memory_space=pltpu.VMEM)
     smem = pl.BlockSpec(memory_space=pltpu.SMEM)
     hbm = pl.BlockSpec(memory_space=pltpu.HBM)
-    plane = (grid_rows // 2, grid_cols // 2)
+    plane = (grid_cols // 2, grid_rows // 2)
     intensity, own, rim = pl.pallas_call(
         body,
         out_shape=(
@@ -454,14 +471,14 @@
         out_specs=(vmem, vmem, vmem),
         scratch_shapes=[
             pltpu.VMEM((kernels, 8) + plane, jnp.float32),
-            pltpu.VMEM((kernels, 2 * rows, cols), jnp.float32),
+            pltpu.VMEM((kernels, 2 * cols, rows), jnp.float32),
             pltpu.VMEM((8,) + plane, jnp.float32),
-            pltpu.VMEM((GROUPS, rows, cols), jnp.float32),
-            pltpu.VMEM((GROUPS, rows, cols), jnp.float32),
+            pltpu.VMEM((GROUPS, cols, rows), jnp.float32),
+            pltpu.VMEM((GROUPS, cols, rows), jnp.float32),
             pltpu.VMEM(kernel_taps.shape, jnp.float32),
-            pltpu.VMEM((2, grid_rows, cols), jnp.float32),
+            pltpu.VMEM((2, rows + taps, cols), jnp.float32),
             pltpu.VMEM((rows, cols), jnp.int32),
-            pltpu.VMEM((2, grid_rows, cols), jnp.float32),
+            pltpu.VMEM((2, rows + taps, cols), jnp.float32),
             pltpu.VMEM((2, 2, RMAX, cols), jnp.float32),
         ]
         + [pltpu.VMEM(t.shape, t.dtype) for t in consts]

time: 37.6 us -> 29.4 us (0.78)
  Pallas kernels: 36.8 us -> 28.6 us
    pallas_call x1, Pallas kernels: 35 us -> 26.8 us  [on_device(): pl.pallas_call(body, out_shape=(jax.ShapeDtypeStruct((GROUPS, rows, cols)...]
where the time goes in v2:
time: 29.4 us; the launch traced here: 29.3 us
  Pallas kernels  28.6 us (97%)
  between operations  0.64 us (2%)
    pallas_call x1, Pallas kernels, on_device(): pl.pallas_call(body, out_shape=(jax.ShapeDtypeStruct((GROUPS, rows, cols)...  26.8 us
    pallas_call x1, Pallas kernels, on_device(): pl.pallas_call(finish, out_shape=(jax.ShapeDtypeStruct((GROUPS, rows, col...  1.81 us

profile of v2, /device:TPU:1, one launch (start us, length us, event | category | flops | bytes accessed | tf_op | source)
XLA Modules:
  0.0 29.3 jit_solution(3070867402230181435)
XLA Ops:
  0.6 26.8 %litho.1 = (f32[3,128,128]{2,1,0:T(8,128)}, f32[2,128,128]{2,1,0:T(8,128)}, f32[2,128,128]{2,1,0:T(8,128)}) custom-call(s32[24]{0:T(128)} %radii_ref.1, s32[24]{0:T(128)} %group_ref.1, f32[24]{0:T(128)} %weight_ref.1, f32[24,2,128,128]{3,2,1,0:T(8,128)} %taps_hbm.1, f32[2,128,128]{2,1,0:T(8,128)} %mask_hbm.1, s32[128,128]{1,0:T(8,128)} %target_hbm.1, ...), custom_call_target="tpu_custom_call" | custom-call | tf_op jit(solution)/shard_map/litho/pallas_call | solution.py:463
  27.5 1.8 %finish.1 = (f32[3,128,128]{2,1,0:T(8,128)}, f32[2,128,128]{2,1,0:T(8,128)}) custom-call(f32[3,128,128]{2,1,0:T(8,128)} %get-tuple-element.5.power_ref, f32[2,128,128]{2,1,0:T(8,128)} %get-tuple-element.6.own_ref, f32[2,128,128]{2,1,0:T(8,128)} %get-tuple-element.7.rim_ref), custom_call_target="tpu_custom_call" | custom-call | tf_op jit(solution)/shard_map/finish/pallas_call | solution.py:496

commit v3 on v2

--- a/solution.py
+++ b/solution.py
@@ -11,7 +11,7 @@
 GROUPS = 3
 STEEPNESS = 1.0
 THRESHOLD = 2.0
-UNROLL = (4, 6, 6)
+UNROLL = (12, 12, 12)
 TABLES = 13
 MESH = pl.DeviceIdType.MESH
 

time: 29.4 us -> 26.6 us (0.905)
  Pallas kernels: 28.6 us -> 25.7 us
    pallas_call x1, Pallas kernels: 26.8 us -> 23.9 us  [on_device(): pl.pallas_call(body, out_shape=(jax.ShapeDtypeStruct((GROUPS, rows, cols)...]
where the time goes in v3:
time: 26.6 us; the launch traced here: 26.4 us
  Pallas kernels  25.7 us (97%)
  between operations  0.64 us (2%)
    pallas_call x1, Pallas kernels, on_device(): pl.pallas_call(body, out_shape=(jax.ShapeDtypeStruct((GROUPS, rows, cols)...  23.9 us
    pallas_call x1, Pallas kernels, on_device(): pl.pallas_call(finish, out_shape=(jax.ShapeDtypeStruct((GROUPS, rows, col...  1.81 us

profile of v3, /device:TPU:1, one launch (start us, length us, event | category | flops | bytes accessed | tf_op | source)
XLA Modules:
  0.0 26.4 jit_solution(6529249997250736747)
XLA Ops:
  0.6 23.9 %litho.1 = (f32[3,128,128]{2,1,0:T(8,128)}, f32[2,128,128]{2,1,0:T(8,128)}, f32[2,128,128]{2,1,0:T(8,128)}) custom-call(s32[24]{0:T(128)} %radii_ref.1, s32[24]{0:T(128)} %group_ref.1, f32[24]{0:T(128)} %weight_ref.1, f32[24,2,128,128]{3,2,1,0:T(8,128)} %taps_hbm.1, f32[2,128,128]{2,1,0:T(8,128)} %mask_hbm.1, s32[128,128]{1,0:T(8,128)} %target_hbm.1, ...), custom_call_target="tpu_custom_call" | custom-call | tf_op jit(solution)/shard_map/litho/pallas_call | solution.py:463
  24.6 1.8 %finish.1 = (f32[3,128,128]{2,1,0:T(8,128)}, f32[2,128,128]{2,1,0:T(8,128)}) custom-call(f32[3,128,128]{2,1,0:T(8,128)} %get-tuple-element.5.power_ref, f32[2,128,128]{2,1,0:T(8,128)} %get-tuple-element.6.own_ref, f32[2,128,128]{2,1,0:T(8,128)} %get-tuple-element.7.rim_ref), custom_call_target="tpu_custom_call" | custom-call | tf_op jit(solution)/shard_map/finish/pallas_call | solution.py:496

commit v4 on v3

--- a/solution.py
+++ b/solution.py
@@ -11,7 +11,7 @@
 GROUPS = 3
 STEEPNESS = 1.0
 THRESHOLD = 2.0
-UNROLL = (12, 12, 12)
+UNROLL = (12, 24, 24)
 TABLES = 13
 MESH = pl.DeviceIdType.MESH
 

time: 26.6 us -> 25.7 us (0.966)
  Pallas kernels: 25.7 us -> 24.9 us
    pallas_call x1, Pallas kernels: 23.9 us -> 23.1 us  [on_device(): pl.pallas_call(body, out_shape=(jax.ShapeDtypeStruct((GROUPS, rows, cols)...]
where the time goes in v4:
time: 25.7 us; the launch traced here: 25.5 us
  Pallas kernels  24.9 us (97%)
  between operations  0.64 us (2%)
    pallas_call x1, Pallas kernels, on_device(): pl.pallas_call(body, out_shape=(jax.ShapeDtypeStruct((GROUPS, rows, cols)...  23.1 us
    pallas_call x1, Pallas kernels, on_device(): pl.pallas_call(finish, out_shape=(jax.ShapeDtypeStruct((GROUPS, rows, col...  1.81 us

profile of v4, /device:TPU:1, one launch (start us, length us, event | category | flops | bytes accessed | tf_op | source)
XLA Modules:
  0.0 25.5 jit_solution(5075155511416600453)
XLA Ops:
  0.6 23.1 %litho.1 = (f32[3,128,128]{2,1,0:T(8,128)}, f32[2,128,128]{2,1,0:T(8,128)}, f32[2,128,128]{2,1,0:T(8,128)}) custom-call(s32[24]{0:T(128)} %radii_ref.1, s32[24]{0:T(128)} %group_ref.1, f32[24]{0:T(128)} %weight_ref.1, f32[24,2,128,128]{3,2,1,0:T(8,128)} %taps_hbm.1, f32[2,128,128]{2,1,0:T(8,128)} %mask_hbm.1, s32[128,128]{1,0:T(8,128)} %target_hbm.1, ...), custom_call_target="tpu_custom_call" | custom-call | tf_op jit(solution)/shard_map/litho/pallas_call | solution.py:463
  23.7 1.8 %finish.1 = (f32[3,128,128]{2,1,0:T(8,128)}, f32[2,128,128]{2,1,0:T(8,128)}) custom-call(f32[3,128,128]{2,1,0:T(8,128)} %get-tuple-element.5.power_ref, f32[2,128,128]{2,1,0:T(8,128)} %get-tuple-element.6.own_ref, f32[2,128,128]{2,1,0:T(8,128)} %get-tuple-element.7.rim_ref), custom_call_target="tpu_custom_call" | custom-call | tf_op jit(solution)/shard_map/finish/pallas_call | solution.py:496

commit v5 on v4

--- a/solution.py
+++ b/solution.py
@@ -276,8 +276,6 @@
     def _():
         pl.semaphore_signal(barrier, inc=1, device_id=next_id, device_id_type=MESH)
 
-    pl.semaphore_wait(barrier, has_prev.astype(jnp.int32) + has_next.astype(jnp.int32))
-
     def exchange(first, src_up, dst_up, src_down, dst_down):
         down = pltpu.make_async_remote_copy(
             src_ref=src_down,
@@ -328,8 +326,6 @@
         mask_hbm.at[:, pl.ds(rows - RMAX, RMAX)],
         ext_ref.at[:, pl.ds(0, RMAX)],
     )
-    start_both(halo)
-
     @pl.when(jnp.logical_not(has_prev))
     def _():
         ext_ref[:, :RMAX] = jnp.zeros_like(ext_ref[:, :RMAX])
@@ -365,7 +361,10 @@
             spectrum(step * UNROLL[0] + i)
         return carry
 
-    lax.fori_loop(0, kernels // UNROLL[0], batch, 0)
+    lax.fori_loop(0, 1, batch, 0)
+    pl.semaphore_wait(barrier, has_prev.astype(jnp.int32) + has_next.astype(jnp.int32))
+    start_both(halo)
+    lax.fori_loop(1, kernels // UNROLL[0], batch, 0)
 
     load_mask.wait()
     load_target.wait()

time: 25.7 us -> 25.6 us (level)
  no operation moved by 1% of the time
where the time goes in v5:
time: 25.6 us; the launch traced here: 25.5 us
  Pallas kernels  24.8 us (97%)
  between operations  0.64 us (2%)
    pallas_call x1, Pallas kernels, on_device(): pl.pallas_call(body, out_shape=(jax.ShapeDtypeStruct((GROUPS, rows, cols)...  23 us
    pallas_call x1, Pallas kernels, on_device(): pl.pallas_call(finish, out_shape=(jax.ShapeDtypeStruct((GROUPS, rows, col...  1.81 us

profile of v5, /device:TPU:1, one launch (start us, length us, event | category | flops | bytes accessed | tf_op | source)
XLA Modules:
  0.0 25.5 jit_solution(17206685797379877786)
XLA Ops:
  0.6 23.0 %litho.1 = (f32[3,128,128]{2,1,0:T(8,128)}, f32[2,128,128]{2,1,0:T(8,128)}, f32[2,128,128]{2,1,0:T(8,128)}) custom-call(s32[24]{0:T(128)} %radii_ref.1, s32[24]{0:T(128)} %group_ref.1, f32[24]{0:T(128)} %weight_ref.1, f32[24,2,128,128]{3,2,1,0:T(8,128)} %taps_hbm.1, f32[2,128,128]{2,1,0:T(8,128)} %mask_hbm.1, s32[128,128]{1,0:T(8,128)} %target_hbm.1, ...), custom_call_target="tpu_custom_call" | custom-call | tf_op jit(solution)/shard_map/litho/pallas_call | solution.py:462
  23.7 1.8 %finish.1 = (f32[3,128,128]{2,1,0:T(8,128)}, f32[2,128,128]{2,1,0:T(8,128)}) custom-call(f32[3,128,128]{2,1,0:T(8,128)} %get-tuple-element.5.power_ref, f32[2,128,128]{2,1,0:T(8,128)} %get-tuple-element.6.own_ref, f32[2,128,128]{2,1,0:T(8,128)} %get-tuple-element.7.rim_ref), custom_call_target="tpu_custom_call" | custom-call | tf_op jit(solution)/shard_map/finish/pallas_call | solution.py:495
